TPU v7x, 32 devices: a whole 2x2x4 slice. The times are simulated.
32 devices in a mesh: comp: 4 (over z), tile: 8 (over y, x, core).
Axes of the slice: x: 2, y: 2, z: 4, core: 2. Of those that a mesh axis runs over, the one named last changes fastest.
Arguments:
- coupled_state: float32 [4, 640, 48, 128], P('comp', None, 'tile'), may hold values from -6 to 6
- diffusivity: float32 [4, 640], P('comp'), may hold values from 0.02 to 0.24
- coupling: bfloat16 [4, 4, 640, 640], P('comp'), may hold values from -0.25 to 0.25
- regrid_weights: bfloat16 [4, 8, 6, 768, 768], P('comp', 'tile'), may hold values from -0.09375 to 0.09375
- source_offsets: int32 [4, 8, 6], P('comp', 'tile'), may hold values from -3 to 3, as said below
- sea_mask: int32 [4, 48, 128], P('comp', 'tile'), may hold values 0 or 1
Outputs:
- coupled_next: float32 [4, 640, 48, 128], P('comp', None, 'tile')
Inputs may be any that keep to these rules, and one draw needn't show every extreme that they name: `source_offsets`: the 6 offsets of one target tile are distinct.
All inputs are finite; a program needn't handle non-finite values. No bound on the sum of `sea_mask` on one device may be relied on, other than what follows from the above.
Results may differ from a plain program's by a relative error of at most 0.0042.
Values may be sent and summed in bfloat16 or wider, within the bound.
A program may use at most 192 MiB of HBM per device.

v0:
```python
import jax
import jax.numpy as jnp
from jax import lax
from jax.sharding import PartitionSpec as P

SWEEPS = 4


section_links = ((0, 0, 1, 1), (0, 0, 1, 1), (1, 1, 0, 1), (0, 0, 1, 0))


def as_sent(value):
    return jax.tree.map(lambda a: a.astype(jnp.bfloat16) if a.dtype == jnp.float32 else a, value)


def with_halo(block, sides, width):
    for axis, dim in sides:
        count = lax.axis_size(axis)
        forward = [(i, i + 1) for i in range(count - 1)]
        forward.append((count - 1, 0))
        backward = [(target, source) for source, target in forward]
        low = lax.ppermute(
            lax.slice_in_dim(block, block.shape[dim] - width, None, axis=dim), axis, forward
        )
        high = lax.ppermute(lax.slice_in_dim(block, 0, width, axis=dim), axis, backward)
        block = jnp.concatenate([low, block, high], axis=dim)
    return block


def sweep_inner(padded, rate_col):
    interior = padded[:, 1:-1, :]
    beside = jnp.pad(interior, ((0, 0), (0, 0), (1, 1)))
    laplacian = (
        padded[:, 2:, :] + padded[:, :-2, :] + beside[:, :, 2:] + beside[:, :, :-2] - 4.0 * interior
    )
    return interior + rate_col * laplacian


def project_for(target_list, slot_count):

    def run(operands):
        weights, lowered = operands
        empty = jnp.zeros((weights.shape[1], lowered.shape[1]), jnp.bfloat16)
        pieces = [empty] * slot_count
        for target in target_list:
            pieces[target] = jnp.dot(
                weights[target], lowered, preferred_element_type=jnp.float32
            ).astype(jnp.bfloat16)
        return jnp.stack(pieces, axis=0)

    return run


def shards(coupled_state, diffusivity, coupling, regrid_weights, source_offsets, sea_mask):
    field_now = coupled_state[0]
    channels, rows_here, columns = field_now.shape
    cell_count = rows_here * columns
    slot_index = lax.axis_index("comp")
    slot_count = lax.axis_size("comp")
    lowered = field_now.astype(jnp.bfloat16).reshape(channels, cell_count)
    target_lists = [
        [target for target in range(slot_count) if section_links[source][target] == 1]
        for source in range(slot_count)
    ]
    branches = [project_for(target_list, slot_count) for target_list in target_lists]
    outgoing = lax.switch(slot_index, branches, (coupling[0], lowered))
    arrived = jax.tree.map(
        lambda part, own: part.astype(own.dtype),
        lax.all_to_all(as_sent(outgoing), "comp", split_axis=0, concat_axis=0, tiled=True),
        outgoing,
    )
    forcing = jnp.sum(arrived.astype(jnp.float32), axis=0).astype(jnp.bfloat16)
    stepped = field_now
    rate_col = diffusivity[0][:, None, None]
    for sweep_index in range(SWEEPS):
        padded = with_halo(stepped, (("tile", 1),), 1)
        stepped = sweep_inner(padded, rate_col)
    tile_index = lax.axis_index("tile")
    tile_count = lax.axis_size("tile")
    offsets_here = source_offsets[0, 0]
    weights_here = regrid_weights[0, 0]
    source_tiles = (tile_index + offsets_here) % tile_count
    initial = jnp.zeros((offsets_here.shape[0], channels, cell_count), jnp.float32)
    tile_piece = lax.all_gather(forcing[None], "tile", axis=0, tiled=True)
    piece_rows = tile_piece.shape[0]
    position = jnp.arange(piece_rows, dtype=jnp.int32)
    matches = (source_tiles[:, None] == position[None, :]).astype(jnp.bfloat16)
    picked = initial + jnp.einsum(
        "kn,ncx->kcx", matches, tile_piece, preferred_element_type=jnp.float32
    )
    regridded = jnp.einsum(
        "kcx,kyx->cy", picked.astype(jnp.bfloat16), weights_here, preferred_element_type=jnp.float32
    )
    update = stepped + regridded.reshape(channels, rows_here, columns)
    active_cells = sea_mask[0][None, :, :] == 1
    return jnp.where(active_cells, update, field_now)[None]


def solution(mesh):
    in_specs = (
        P("comp", None, "tile", None),
        P("comp", None),
        P("comp", None, None, None),
        P("comp", "tile", None, None, None),
        P("comp", "tile", None),
        P("comp", "tile", None),
    )
    out_specs = P("comp", None, "tile", None)
    return jax.shard_map(shards, mesh=mesh, in_specs=in_specs, out_specs=out_specs, check_vma=False)
```

profile of v0, /device:TPU:24, one launch (start us, length us, event | category | flops | bytes accessed | tf_op | source)
XLA Modules:
  0.0 208.4 jit_solution(6749385750106683561)
XLA Ops:
  6.5 1.8 copy.9
  8.3 4.5 %conditional.1 = (bf16[4,640,768]{2,1,0:T(8,128)(2,1)}) conditional(s32[]{:T(128)} %clamp.3, (bf16[4,640,640]{2,1,0:T(8,128)(2,1)}, bf16[640,768]{0,1:T(8,128)(2,1)S(1)}) %tuple.36, (bf16[4,640,640]{2,1,0:T(8,128)(2,1)}, bf16[640,768]{0,1:T(8,128)(2,1)S(1)}) %tuple.37, (bf16[4,640,640]{2,1,0:T(8,128)(2,1)}, ...), branch_computations={%region_0.0_spmd, %region_1.0_spmd, %region_2.0_spmd, %region_3.0_... | conditional | flops 1894809600 | bytes 28344376 | solution.py:66
  8.3 2.1 %fusion.21 = bf16[1,640,768]{2,1,0:T(8,128)(2,1)S(1)} fusion(bf16[640,768]{0,1:T(8,128)(2,1)S(1)} %get-tuple-element.41, bf16[4,640,640]{2,1,0:T(8,128)(2,1)} %get-tuple-element.32), kind=kOutput, calls=%fused_computation.33 | convolution fusion | flops 629637120 | bytes 2785280 | tf_op jit(solution)/shard_map/cond/branch_3_fun/dot_general | solution.py:46
  10.5 2.2 %maximum_maximum_fusion = bf16[4,640,768]{2,1,0:T(8,128)(2,1)} fusion(bf16[1,640,768]{2,1,0:T(8,128)(2,1)S(1)} %fusion.21, bf16[4]{0:T(256)(128)(2,1)S(1)} %pad.29.clone, bf16[4]{0:T(256)(128)(2,1)S(1)} %pad.27.clone), kind=kLoop, calls=%fused_computation.31 | loop fusion | flops 3932160 | bytes 4915216 | tf_op jit(solution)/shard_map/cond/branch_3_fun/stack | solution.py:49
  12.8 92.9 %all_to_all.5 = bf16[4,640,768]{2,1,0:T(8,128)(2,1)} all-to-all(bf16[4,640,768]{2,1,0:T(8,128)(2,1)} %get-tuple-element.50), channel_id=1, replica_groups=mesh['comp'=4,'tile'=8] {'comp'}, dimensions={0} | all-to-all | bytes 7864320 | tf_op jit(solution)/shard_map/all_to_all | solution.py:69
  105.6 4.1 %reduce_sum.12 = bf16[640,768]{1,0:T(8,128)(2,1)} reduce(bf16[4,640,768]{2,1,0:T(8,128)(2,1)} %all_to_all.5, bf16[]{:T(256)} %constant.43.clone.1), dimensions={0}, to_apply=%region_4.0 | reduce | flops 1474560 | bytes 4915202 | tf_op jit(solution)/shard_map/reduce_sum | solution.py:72
  109.8 1.9 collective-permute-start
  111.7 7.6 %collective-permute-done = f32[640,1,128]{2,0,1:T(8,128)S(1)} collective-permute-done((f32[640,1,128]{2,0,1:T(8,128)S(1)}, f32[640,1,128]{2,0,1:T(8,128)S(1)}, u32[]{:S(2)}, u32[]{:S(2)}) %collective-permute-start) | collective-permute-done | bytes 327712 | tf_op jit(solution)/shard_map/ppermute | solution.py:25
  119.3 1.9 collective-permute-done.1
  121.3 1.2 fusion.33
  122.5 0.9 collective-permute-start.2
  123.4 13.8 %collective-permute-done.2 = f32[640,1,128]{2,0,1:T(8,128)S(1)} collective-permute-done((f32[640,1,128]{2,0,1:T(8,128)S(1)}, f32[640,1,128]{2,0,1:T(8,128)S(1)}, u32[]{:S(2)}, u32[]{:S(2)}) %collective-permute-start.2) | collective-permute-done | bytes 327712 | tf_op jit(solution)/shard_map/ppermute | solution.py:25
  137.3 2.8 %collective-permute-done.3 = f32[640,1,128]{2,0,1:T(8,128)S(1)} collective-permute-done((f32[640,1,128]{2,0,1:T(8,128)S(1)}, f32[640,1,128]{2,0,1:T(8,128)S(1)}, u32[]{:S(2)}, u32[]{:S(2)}) %collective-permute-start.3) | collective-permute-done | bytes 327712 | tf_op jit(solution)/shard_map/ppermute | solution.py:22
  140.1 1.2 fusion.38
  141.3 1.3 copy-done.1
  142.7 0.5 collective-permute-start.5
  143.2 13.2 %collective-permute-done.4 = f32[640,1,128]{2,0,1:T(8,128)S(1)} collective-permute-done((f32[640,1,128]{2,0,1:T(8,128)S(1)}, f32[640,1,128]{2,0,1:T(8,128)S(1)}, u32[]{:S(2)}, u32[]{:S(2)}) %collective-permute-start.4) | collective-permute-done | bytes 327712 | tf_op jit(solution)/shard_map/ppermute | solution.py:25
  156.4 1.0 collective-permute-done.5
  157.4 5.5 %fusion.43 = f32[640,6,128]{2,0,1:T(8,128)S(1)} fusion(f32[640,6,128]{2,0,1:T(8,128)} %copy-done.1, f32[640,1,128]{2,0,1:T(8,128)S(1)} %collective-permute-done.5, f32[640,1,128]{2,0,1:T(8,128)S(1)} %collective-permute-done.4, f32[640]{0:T(1024)S(1)} %reduce.1), kind=kLoop, calls=%fused_computation.63 | loop fusion | flops 4423680 | bytes 4590080 | tf_op jit(solution)/shard_map/add | solution.py:36
  163.0 1.3 copy-done.2
  164.3 2.1 collective-permute-start.6
  166.4 11.0 %all-gather.3.cloned.1.call-done = bf16[5120,768]{1,0:T(8,128)(2,1)} async-done(((bf16[640,768]{1,0:T(8,128)(2,1)}), bf16[5120,768]{1,0:T(8,128)(2,1)}) %all-gather.3.cloned.1.call-update) | async-done | bytes 7864336 | tf_op jit(solution)/shard_map/all_gather | solution.py:84
  177.4 11.2 %fusion.24 = bf16[6,640,768]{2,0,1:T(8,128)(2,1)} fusion(bf16[8,640,768]{2,1,0:T(8,128)(2,1)} %bitcast.85, s32[6]{0:T(128)S(1)} %and_select_fusion), kind=kOutput, calls=%fused_computation.37 | convolution fusion | flops 47185968 | bytes 13762584 | tf_op jit(solution)/shard_map/kn,ncx->kcx/dot_general | solution.py:88
  188.6 13.0 %fusion.51 = f32[1,640,6,128]{3,1,2,0:T(8,128)} fusion(f32[640,6,128]{2,0,1:T(8,128)S(1)} %copy-done.3, f32[640,1,128]{2,0,1:T(8,128)S(1)} %collective-permute-done.7, f32[640,1,128]{2,0,1:T(8,128)S(1)} %collective-permute-done.6, bf16[6,128,6,768]{3,1,0,2:T(8,128)(2,1)} %bitcast.91, bf16[6,640,768]{2,0,1:T(8,128)(2,1)} %fusion.24, f32[640]{0:T(1024)S(1)} %reduce.1, ...), kind=kOutput, calls=%fused_computation.71 | convolution fusion | flops 4535255040 | bytes 19533056 | tf_op jit(solution)/shard_map/kcx,kyx->cy/dot_general | solution.py:91
  (31 shorter events, 0.4 us)
Async XLA Ops:
  6.5 170.8 %all-gather.3.cloned.1.call-start = ((), (), s32[]{:S(2)}) async-start(), calls=%async_computation.1 | async-start | bytes 8847360 | tf_op jit(solution)/shard_map/all_gather | solution.py:84
  105.6 4.1 %copy-start = (f32[1,640,6,128]{3,1,2,0:T(8,128)S(1)}, f32[1,640,6,128]{3,1,2,0:T(8,128)}, u32[]{:S(2)}) copy-start(f32[1,640,6,128]{3,1,2,0:T(8,128)} %param.10) | copy-start | bytes 5898244
  109.7 2.0 copy-start.5
  109.8 9.5 %collective-permute-start = (f32[640,1,128]{2,0,1:T(8,128)S(1)}, f32[640,1,128]{2,0,1:T(8,128)S(1)}, u32[]{:S(2)}, u32[]{:S(2)}) collective-permute-start(f32[640,1,128]{2,0,1:T(8,128)S(1)} %get-tuple-element.48), channel_id=1, source_target_pairs={{1,0},{2,1},{3,2},{4,3},{5,4},{6,5},{7,6},{0,7},{9,8},{10,9},{11,1... | collective-permute-start | bytes 983048 | tf_op jit(solution)/shard_map/ppermute | solution.py:25
  111.7 9.6 %collective-permute-start.1 = (f32[640,1,128]{2,0,1:T(8,128)S(1)}, f32[640,1,128]{2,0,1:T(8,128)S(1)}, u32[]{:S(2)}, u32[]{:S(2)}) collective-permute-start(f32[640,1,128]{2,0,1:T(8,128)S(1)} %get-tuple-element.49), channel_id=1, source_target_pairs={{0,1},{1,2},{2,3},{3,4},{4,5},{5,6},{6,7},{7,0},{8,9},{9,10},{10,1... | collective-permute-start | bytes 983048 | tf_op jit(solution)/shard_map/ppermute | solution.py:22
  122.5 14.8 %collective-permute-start.2 = (f32[640,1,128]{2,0,1:T(8,128)S(1)}, f32[640,1,128]{2,0,1:T(8,128)S(1)}, u32[]{:S(2)}, u32[]{:S(2)}) collective-permute-start(f32[640,1,128]{2,0,1:T(8,128)S(1)} %get-tuple-element.46), channel_id=1, source_target_pairs={{1,0},{2,1},{3,2},{4,3},{5,4},{6,5},{7,6},{0,7},{9,8},{10,9},{11,1... | collective-permute-start | bytes 983048 | tf_op jit(solution)/shard_map/ppermute | solution.py:25
  123.4 19.7 %copy-start.4 = (s32[1,6,128]{2,0,1:T(1,128)S(1)}, s32[1,6,128]{2,0,1:T(1,128)}, u32[]{:S(2)}) copy-start(s32[1,6,128]{2,0,1:T(1,128)} %param.15) | copy-start | bytes 9220
  123.4 19.8 %copy-start.7 = (s32[1,1,6]{2,1,0:T(1,128)S(1)}, s32[1,1,6]{2,1,0:T(1,128)}, u32[]{:S(2)}) copy-start(s32[1,1,6]{2,1,0:T(1,128)} %param.14) | copy-start | bytes 76
  123.4 16.7 %collective-permute-start.3 = (f32[640,1,128]{2,0,1:T(8,128)S(1)}, f32[640,1,128]{2,0,1:T(8,128)S(1)}, u32[]{:S(2)}, u32[]{:S(2)}) collective-permute-start(f32[640,1,128]{2,0,1:T(8,128)S(1)} %get-tuple-element.47), channel_id=1, source_target_pairs={{0,1},{1,2},{2,3},{3,4},{4,5},{5,6},{6,7},{7,0},{8,9},{9,10},{10,1... | collective-permute-start | bytes 983048 | tf_op jit(solution)/shard_map/ppermute | solution.py:22
  141.3 1.3 copy-start.1
  142.6 13.8 %collective-permute-start.4 = (f32[640,1,128]{2,0,1:T(8,128)S(1)}, f32[640,1,128]{2,0,1:T(8,128)S(1)}, u32[]{:S(2)}, u32[]{:S(2)}) collective-permute-start(f32[640,1,128]{2,0,1:T(8,128)S(1)} %get-tuple-element.44), channel_id=1, source_target_pairs={{1,0},{2,1},{3,2},{4,3},{5,4},{6,5},{7,6},{0,7},{9,8},{10,9},{11,1... | collective-permute-start | bytes 983048 | tf_op jit(solution)/shard_map/ppermute | solution.py:25
  142.7 14.8 %collective-permute-start.5 = (f32[640,1,128]{2,0,1:T(8,128)S(1)}, f32[640,1,128]{2,0,1:T(8,128)S(1)}, u32[]{:S(2)}, u32[]{:S(2)}) collective-permute-start(f32[640,1,128]{2,0,1:T(8,128)S(1)} %get-tuple-element.45), channel_id=1, source_target_pairs={{0,1},{1,2},{2,3},{3,4},{4,5},{5,6},{6,7},{7,0},{8,9},{9,10},{10,1... | collective-permute-start | bytes 983048 | tf_op jit(solution)/shard_map/ppermute | solution.py:22
  163.0 1.3 copy-start.2
  164.3 24.3 %collective-permute-start.6 = (f32[640,1,128]{2,0,1:T(8,128)S(1)}, f32[640,1,128]{2,0,1:T(8,128)S(1)}, u32[]{:S(2)}, u32[]{:S(2)}) collective-permute-start(f32[640,1,128]{2,0,1:T(8,128)S(1)} %get-tuple-element.42), channel_id=1, source_target_pairs={{1,0},{2,1},{3,2},{4,3},{5,4},{6,5},{7,6},{0,7},{9,8},{10,9},{11,1... | collective-permute-start | bytes 983048 | tf_op jit(solution)/shard_map/ppermute | solution.py:25
  166.4 22.2 %collective-permute-start.7 = (f32[640,1,128]{2,0,1:T(8,128)S(1)}, f32[640,1,128]{2,0,1:T(8,128)S(1)}, u32[]{:S(2)}, u32[]{:S(2)}) collective-permute-start(f32[640,1,128]{2,0,1:T(8,128)S(1)} %get-tuple-element.43), channel_id=1, source_target_pairs={{0,1},{1,2},{2,3},{3,4},{4,5},{5,6},{6,7},{7,0},{8,9},{9,10},{10,1... | collective-permute-start | bytes 983048 | tf_op jit(solution)/shard_map/ppermute | solution.py:22
  177.4 11.2 %copy-start.3 = (f32[640,6,128]{2,0,1:T(8,128)S(1)}, f32[640,6,128]{2,0,1:T(8,128)}, u32[]{:S(2)}) copy-start(f32[640,6,128]{2,0,1:T(8,128)} %copy-done.2) | copy-start | bytes 5898244
Sparse Core Ops, SparseCore 0:
  109.9 67.4 all-gather.2
where the time goes:
time: 212 us; the launch traced here: 208 us
  blocking collectives  92.9 us (44%)
  waiting for transfers between devices  51.5 us (24%)
  matrix products  26.3 us (12%)
  other arithmetic  14.2 us (7%)
  between operations  13.5 us (6%)
  starting transfers between devices  5.45 us (3%)
  local copies, waits for them, and re-layouts  4.57 us (2%)
    all_to_all x1, blocking collectives, shards(): lax.all_to_all(as_sent(outgoing), 'comp', split_axis=0, concat_axis=0, ti...  92.9 us
    ppermute x4, waiting for transfers between devices, with_halo(): lax.ppermute(lax.slice_in_dim(block, 0, width, axis=dim), axis, backward)  34.7 us
    dot_general x1, matrix products, shards(): jnp.einsum('kcx,kyx->cy', picked.astype(jnp.bfloat16), weights_here, pref...  13 us
    dot_general x1, matrix products, shards(): jnp.einsum('kn,ncx->kcx', matches, tile_piece, preferred_element_type=jnp...  11.2 us
    all_gather x1, waiting for transfers between devices, shards(): tile_piece = lax.all_gather(forcing[None], 'tile', axis=0, tiled=True)  11 us
    add x3, other arithmetic, sweep_inner(): return interior + rate_col * laplacian  7.84 us
    ppermute x4, waiting for transfers between devices, with_halo(): lax.ppermute(lax.slice_in_dim(block, block.shape[dim] - width, None, axis...  5.79 us
    ppermute x4, starting transfers between devices, with_halo(): lax.ppermute(lax.slice_in_dim(block, 0, width, axis=dim), axis, backward)  4.96 us
  transfers between devices with their start and end apart: 9, of which 7 were waited for; matrix products, arithmetic and copies ran while one was open for 9% of the time, Pallas kernels for 0%

commit v1 on v0

v1 whole, which is shorter than its diff:
```python
import functools

import jax
import jax.numpy as jnp
from jax import lax
from jax.experimental import pallas as pl
from jax.experimental.pallas import tpu as pltpu
from jax.sharding import PartitionSpec as P

SWEEPS = 4
REACH = 3
CHUNK = 64
MESH = pl.DeviceIdType.MESH


def flip(index, bit):
    return index + bit - 2 * bit * lax.rem(lax.div(index, bit), 2)


def body(
    slots, tiles, chunk,
    x_ref, diff_ref, coup_ref, regw_ref, off_ref, mask_ref,
    out_ref,
    xb, rate, cbuf, wbuf, gbuf, pbuf, abuf, fbuf, halo,
    csend, crecv, hsend, hrecv, gsend, grecv, lsem,
):
    s = lax.axis_index("comp")
    t = lax.axis_index("tile")
    rows_here, channels, columns = x_ref.shape
    pairs = regw_ref.shape[0]
    edge = SWEEPS * columns
    cells = rows_here * columns
    count = channels // chunk
    half = chunk // 2
    paired = tiles == 8

    loads = [
        pltpu.make_async_copy(coup_ref.at[3 - lax.div(s, 3)], cbuf.at[0], lsem.at[0]),
        pltpu.make_async_copy(coup_ref.at[2 - 2 * lax.div(s, 2)], cbuf.at[1], lsem.at[1]),
        pltpu.make_async_copy(coup_ref.at[1], cbuf.at[2], lsem.at[2]),
        pltpu.make_async_copy(regw_ref, wbuf.at[pl.ds(0, pairs)], lsem.at[3]),
    ]
    for load in loads:
        load.start()

    barrier = pltpu.get_barrier_semaphore()
    steps = range(1, tiles) if paired else [d for r in range(1, REACH + 1) for d in (r, tiles - r)]
    greeted = [(lax.rem(s + d, slots), t) for d in range(1, slots)]
    greeted += [(s, lax.rem(t + d, tiles)) for d in steps]
    for other in greeted:
        pl.semaphore_signal(barrier, inc=1, device_id=other, device_id_type=MESH)

    for r in range(rows_here):
        xb[:, r * columns : (r + 1) * columns] = x_ref[r].astype(jnp.bfloat16)
    wbuf[pairs] = jnp.zeros_like(wbuf[pairs])
    for c in range(channels // columns):
        row = jnp.broadcast_to(diff_ref[:, c * columns : (c + 1) * columns], (columns, columns))
        rate[c * columns : (c + 1) * columns, :] = row.T

    pl.semaphore_wait(barrier, len(greeted))

    def send(src, dst, send_sem, recv_sem, where):
        return pltpu.make_async_remote_copy(
            src_ref=src, dst_ref=dst, send_sem=send_sem, recv_sem=recv_sem,
            device_id=where, device_id_type=MESH,
        )

    below = (s, lax.rem(t + 1, tiles))
    above = (s, lax.rem(t + tiles - 1, tiles))
    halos = [
        send(xb.at[:, pl.ds(cells - edge, edge)], halo.at[0], hsend.at[0], hrecv.at[0], below),
        send(xb.at[:, pl.ds(0, edge)], halo.at[1], hsend.at[1], hrecv.at[1], above),
    ]

    def span(i):
        return pl.ds(pl.multiple_of(i * chunk, chunk), chunk)

    def project(which, i):
        pbuf[which, span(i), :] = jnp.dot(
            cbuf[which, span(i), :], xb[...], preferred_element_type=jnp.float32
        ).astype(jnp.bfloat16)

    def to_a(i, where):
        return send(pbuf.at[0, span(i), :], abuf.at[0, span(i), :], csend.at[0, i], crecv.at[0, i], where)

    def to_b(i, where):
        return send(pbuf.at[1, span(i), :], abuf.at[1, span(i), :], csend.at[1, i], crecv.at[1, i], where)

    def to_f(which, i, where):
        return send(
            pbuf.at[which, span(i), :], fbuf.at[span(i), :], csend.at[which, i], crecv.at[2, i], where
        )

    up1 = (lax.rem(s + 1, slots), t)

    def out_copies(section, i):
        if section in (0, 1):
            return [to_a(i, (section + 1, t)), to_b(i, (section + 1, t))]
        if section == 2:
            return [to_f(0, i, (3, t)), to_f(1, i, (0, t)), to_f(2, i, (1, t))]
        return [to_f(0, i, (2, t))]

    near = {b: (s, flip(t, b)) for b in (1, 2, 4)} if paired else {}
    if paired:
        near[5] = (s, flip(flip(t, 4), 1))
        own = 0
        held = (1, 2, 3, 5, 6, 7)
    else:
        own = REACH
        held = tuple(o for o in range(2 * REACH + 1) if o != REACH)

    def first(i):
        return pl.ds(pl.multiple_of(i * chunk, half), half)

    def second(i):
        return pl.ds(pl.multiple_of(i * chunk + half, half), half)

    def relay(n, i, src, dst, part, where):
        return send(
            src.at[part, :], gbuf.at[dst, part, :], gsend.at[n, i], grecv.at[n, i], where
        )

    def gather1(i):
        if paired:
            return [
                relay(0, i, fbuf, 1, span(i), near[1]),
                relay(1, i, fbuf, 2, span(i), near[2]),
                relay(2, i, fbuf, 5, span(i), near[5]),
            ]
        copies = []
        for n, o in enumerate(held):
            d = REACH - o
            copies.append(relay(n, i, fbuf, o, span(i), (s, lax.rem(t + tiles + d, tiles))))
        return copies

    def gather2(i):
        if not paired:
            return []
        return [
            relay(3, i, gbuf.at[2], 3, span(i), near[1]),
            relay(4, i, gbuf.at[2], 6, first(i), near[4]),
            relay(5, i, gbuf.at[5], 7, second(i), near[2]),
        ]

    def gather3(i):
        if not paired:
            return []
        return [
            relay(6, i, gbuf.at[6], 7, first(i), near[1]),
            relay(7, i, gbuf.at[7], 6, second(i), near[1]),
        ]

    def block_of(slot):
        if paired:
            tile = t
            for bit in (1, 2, 4):
                if slot & bit:
                    tile = flip(tile, bit)
            offset = lax.rem(tile - t + tiles + REACH, tiles) - REACH
        else:
            offset = slot - REACH
        found = jnp.int32(pairs)
        for k in range(pairs):
            found = jnp.where(off_ref[0, k] == offset, jnp.int32(k), found)
        return found

    loads[0].wait()
    loads[1].wait()
    loads[2].wait()

    def phase_a(i, carry):
        @pl.when(s == 0)
        def _():
            project(0, i)
            to_a(i, (1, t)).start()
            project(1, i)
            to_b(i, (1, t)).start()

        @pl.when(s == 2)
        def _():
            project(2, i)
            to_f(2, i, (1, t)).start()
            project(1, i)
            to_f(1, i, (0, t)).start()

        @pl.when(s == 3)
        def _():
            project(0, i)
            to_f(0, i, (2, t)).start()

        return carry

    for copy in halos:
        copy.start()
    lax.fori_loop(0, count, phase_a, 0)
    loads[3].wait()
    blocks = {slot: block_of(slot) for slot in (own,) + held}

    def add_to(which, landed, i):
        pbuf[which, span(i), :] = (
            pbuf[which, span(i), :].astype(jnp.float32) + landed[span(i), :].astype(jnp.float32)
        ).astype(jnp.bfloat16)

    def forcing(i):
        @pl.when(s == 1)
        def _():
            project(0, i)
            to_a(i, (2, t)).wait_recv()
            add_to(0, abuf.at[0], i)
            to_a(i, (2, t)).start()
            project(1, i)
            to_b(i, (2, t)).wait_recv()
            add_to(1, abuf.at[1], i)
            to_b(i, (2, t)).start()

        @pl.when(s == 2)
        def _():
            project(0, i)
            to_a(i, (3, t)).wait_recv()
            add_to(0, abuf.at[0], i)
            to_f(0, i, (3, t)).start()
            to_b(i, (3, t)).wait_recv()

        to_f(0, i, up1).wait_recv()

        @pl.when(s == 2)
        def _():
            fbuf[span(i), :] = (
                fbuf[span(i), :].astype(jnp.float32) + abuf[1, span(i), :].astype(jnp.float32)
            ).astype(jnp.bfloat16)

        for copy in gather1(i):
            copy.start()

    def diffuse(i):
        lane = lax.broadcasted_iota(jnp.int32, (16, columns), 1)
        inner_low = lane > 0
        inner_high = lane < columns - 1

        def block(j, carry):
            rows = pl.ds(pl.multiple_of(i * chunk + j * 16, 16), 16)
            scale = rate[rows, :]
            planes = [
                halo[0, rows, r * columns : (r + 1) * columns].astype(jnp.float32) for r in range(SWEEPS)
            ]
            planes += [x_ref[r, rows, :] for r in range(rows_here)]
            planes += [
                halo[1, rows, r * columns : (r + 1) * columns].astype(jnp.float32) for r in range(SWEEPS)
            ]
            for _ in range(SWEEPS):
                fresh = []
                for r in range(1, len(planes) - 1):
                    mid = planes[r]
                    left = jnp.where(inner_low, pltpu.roll(mid, 1, 1), 0.0)
                    right = jnp.where(inner_high, pltpu.roll(mid, columns - 1, 1), 0.0)
                    lap = planes[r + 1] + planes[r - 1] + right + left - 4.0 * mid
                    fresh.append(mid + scale * lap)
                planes = fresh
            for r in range(rows_here):
                out_ref[r, rows, :] = planes[r]
            return carry

        lax.fori_loop(0, chunk // 16, block, 0)

    def finish(i):
        dims = (((1,), (1,)), ((), ()))
        total = lax.dot_general(
            fbuf[span(i), :], wbuf[blocks[own]], dims, preferred_element_type=jnp.float32
        )
        for slot in held:
            total += lax.dot_general(
                gbuf[slot, span(i), :], wbuf[blocks[slot]], dims, preferred_element_type=jnp.float32
            )
        for r in range(rows_here):
            here = total[:, r * columns : (r + 1) * columns]
            out_ref[r, span(i), :] = jnp.where(
                mask_ref[r] == 1, out_ref[r, span(i), :] + here, x_ref[r, span(i), :]
            )

    def phase_b(i, carry):
        @pl.when(i < count)
        def _():
            forcing(i)

        @pl.when((i >= 1) & (i < count + 1))
        def _():
            if paired:
                one = gather1(i - 1)
                two = gather2(i - 1)
                one[1].wait_recv()
                two[0].start()
                two[1].start()
                one[2].wait_recv()
                two[2].start()

        @pl.when(i == 2)
        def _():
            for copy in halos:
                copy.wait_recv()

        @pl.when((i >= 2) & (i < count + 2))
        def _():
            if paired:
                two = gather2(i - 2)
                three = gather3(i - 2)
                two[1].wait_recv()
                three[0].start()
                two[2].wait_recv()
                three[1].start()
            diffuse(i - 2)

        @pl.when(i >= 3)
        def _():
            if paired:
                gather1(i - 3)[0].wait_recv()
                gather2(i - 3)[0].wait_recv()
                for copy in gather3(i - 3):
                    copy.wait_recv()
            else:
                for copy in gather1(i - 3):
                    copy.wait_recv()
            finish(i - 3)

        return carry

    lax.fori_loop(0, count + 3, phase_b, 0)

    def drain(i, carry):
        for section in range(slots):
            @pl.when(s == section)
            def _():
                for copy in out_copies(section, i):
                    copy.wait_send()
        for copy in gather1(i) + gather2(i) + gather3(i):
            copy.wait_send()
        return carry

    lax.fori_loop(0, count, drain, 0)
    for copy in halos:
        copy.wait_send()


def shards(slots, tiles, coupled_state, diffusivity, coupling, regrid_weights, source_offsets, sea_mask):
    _, channels, rows_here, columns = coupled_state.shape
    cells = rows_here * columns
    pairs = regrid_weights.shape[2]
    chunk = CHUNK
    count = channels // chunk
    vmem = pl.BlockSpec(memory_space=pltpu.VMEM)
    smem = pl.BlockSpec(memory_space=pltpu.SMEM)
    anyspace = pl.BlockSpec(memory_space=pl.ANY)
    dma = pltpu.SemaphoreType.DMA
    low = jnp.bfloat16
    held = 8 if tiles == 8 else 2 * REACH + 1
    result = pl.pallas_call(
        functools.partial(body, slots, tiles, chunk),
        out_shape=jax.ShapeDtypeStruct((rows_here, channels, columns), jnp.float32),
        in_specs=[vmem, vmem, anyspace, anyspace, smem, vmem],
        out_specs=vmem,
        scratch_shapes=[
            pltpu.VMEM((channels, cells), low),
            pltpu.VMEM((channels, columns), jnp.float32),
            pltpu.VMEM((3, channels, channels), low),
            pltpu.VMEM((pairs + 1, cells, cells), low),
            pltpu.VMEM((held, channels, cells), low),
            pltpu.VMEM((3, channels, cells), low),
            pltpu.VMEM((2, channels, cells), low),
            pltpu.VMEM((channels, cells), low),
            pltpu.VMEM((2, channels, SWEEPS * columns), low),
            dma((3, count)),
            dma((3, count)),
            dma((2,)),
            dma((2,)),
            dma((8, count)),
            dma((8, count)),
            dma((4,)),
        ],
        compiler_params=pltpu.CompilerParams(
            collective_id=0, has_side_effects=True, vmem_limit_bytes=60 * 1024 * 1024
        ),
        name="exchange",
    )(
        coupled_state[0].transpose(1, 0, 2),
        diffusivity,
        coupling[0],
        regrid_weights[0, 0],
        source_offsets[0],
        sea_mask[0][:, None, :],
    )
    return result.transpose(1, 0, 2)[None]


def solution(mesh):
    in_specs = (
        P("comp", None, "tile", None),
        P("comp", None),
        P("comp", None, None, None),
        P("comp", "tile", None, None, None),
        P("comp", "tile", None),
        P("comp", "tile", None),
    )
    out_specs = P("comp", None, "tile", None)
    run = functools.partial(shards, mesh.shape["comp"], mesh.shape["tile"])
    return jax.shard_map(run, mesh=mesh, in_specs=in_specs, out_specs=out_specs, check_vma=False)
```

time: 212 us -> 86.4 us (0.41); the launches traced: 208 us -> 86.3 us
  blocking collectives: 92.9 us -> 0 us
  Pallas kernels: 0 us -> 83.3 us
  waiting for transfers between devices: 51.5 us -> 0 us
  matrix products: 26.3 us -> 0 us
  other arithmetic: 14.2 us -> 0 us
  between operations: 13.5 us -> 0.01 us
  starting transfers between devices: 5.45 us -> 0 us
    all_to_all x1 -> x0, blocking collectives: 92.9 us -> none  [shards(): lax.all_to_all(as_sent(outgoing), 'comp', split_axis=0, concat_axis=0, ti...]
    pallas_call x0 -> x1, Pallas kernels: none -> 83.3 us  [shards(): pl.pallas_call(functools.partial(body, slots, tiles, chunk), out_shape=ja...]
    ppermute x8 -> x0, waiting for transfers between devices: 40.5 us -> none  [the longest x4 34.7 us: with_halo(): lax.ppermute(lax.slice_in_dim(block, 0, width, axis=dim), axis, backward)]
    dot_general x3 -> x0, matrix products: 26.3 us -> none  [the longest x1 13 us: shards(): jnp.einsum('kcx,kyx->cy', picked.astype(jnp.bfloat16), weights_here, pref...]
    all_gather x1 -> x0, waiting for transfers between devices: 11 us -> none  [shards(): tile_piece = lax.all_gather(forcing[None], 'tile', axis=0, tiled=True)]
    add x3 -> x0, other arithmetic: 7.84 us -> none  [sweep_inner(): return interior + rate_col * laplacian]
    ppermute x8 -> x0, starting transfers between devices: 5.44 us -> none  [the longest x4 4.96 us: with_halo(): lax.ppermute(lax.slice_in_dim(block, 0, width, axis=dim), axis, backward)]
    reduce_sum x1 -> x0, other arithmetic: 4.08 us -> none  [shards(): forcing = jnp.sum(arrived.astype(jnp.float32), axis=0).astype(jnp.bfloat16)]
  transfers between devices with their start and end apart: 9 -> 0, of which waited for: 7 -> 0; matrix products, arithmetic and copies ran while one was open for 9% -> 0% of each run, Pallas kernels for 0% -> 0%
where the time goes in v1:
time: 86.4 us; the launch traced here: 86.3 us
  Pallas kernels  83.3 us (96%)
  local copies, waits for them, and re-layouts  2.94 us (3%)
    pallas_call x1, Pallas kernels, shards(): pl.pallas_call(functools.partial(body, slots, tiles, chunk), out_shape=ja...  83.3 us
    unnamed x1, local copies, waits for them, and re-layouts  2.94 us

profile of v1, /device:TPU:24, one launch (start us, length us, event | category | flops | bytes accessed | tf_op | source)
XLA Modules:
  0.0 86.3 jit_solution(9567048906999747758)
XLA Ops:
  0.0 83.3 %exchange.1 = f32[6,640,128]{2,1,0:T(8,128)} custom-call(f32[6,640,128]{2,1,0:T(8,128)} %bitcast.13, f32[1,640]{1,0:T(1,128)} %diff_ref.1, bf16[4,640,640]{2,1,0:T(8,128)(2,1)} %bitcast.12, bf16[6,768,768]{2,1,0:T(8,128)(2,1)} %bitcast.11, s32[1,6]{1,0:T(1,128)} %bitcast.15, s32[6,1,128]{2,1,0:T(1,128)} %bitcast.14), custom_call_target="tpu_custom_call" | custom-call | tf_op jit(solution)/shard_map/exchange/pallas_call | solution.py:355
  83.3 2.9 %copy.8 = f32[1,640,6,128]{3,1,2,0:T(8,128)} copy(f32[1,640,6,128]{3,1,2,0:T(8,128)} %bitcast.10) | data formatting | bytes 3932160

commit v2 on v1

--- a/solution.py
+++ b/solution.py
@@ -9,7 +9,8 @@
 
 SWEEPS = 4
 REACH = 3
-CHUNK = 64
+CHUNK = 128
+EXTRA = 0
 MESH = pl.DeviceIdType.MESH
 
 
@@ -19,10 +20,10 @@
 
 def body(
     slots, tiles, chunk,
-    x_ref, diff_ref, coup_ref, regw_ref, off_ref, mask_ref,
-    out_ref,
-    xb, rate, cbuf, wbuf, gbuf, pbuf, abuf, fbuf, halo,
-    csend, crecv, hsend, hrecv, gsend, grecv, lsem,
+    xin_ref, diff_ref, coup_ref, regw_ref, off_ref, mask_ref,
+    result_ref,
+    x_ref, out_ref, xb, rate, cbuf, wraw, wbuf, gbuf, pbuf, abuf, fbuf, halo,
+    csend, crecv, hsend, hrecv, gsend, grecv, lsem, osem,
 ):
     s = lax.axis_index("comp")
     t = lax.axis_index("tile")
@@ -31,16 +32,18 @@
     edge = SWEEPS * columns
     cells = rows_here * columns
     count = channels // chunk
-    half = chunk // 2
+    part = chunk * 5 // 8 // 8 * 8
     paired = tiles == 8
 
+    load_x = pltpu.make_async_copy(xin_ref, x_ref, lsem.at[4])
+    load_x.start()
     loads = [
         pltpu.make_async_copy(coup_ref.at[3 - lax.div(s, 3)], cbuf.at[0], lsem.at[0]),
         pltpu.make_async_copy(coup_ref.at[2 - 2 * lax.div(s, 2)], cbuf.at[1], lsem.at[1]),
         pltpu.make_async_copy(coup_ref.at[1], cbuf.at[2], lsem.at[2]),
-        pltpu.make_async_copy(regw_ref, wbuf.at[pl.ds(0, pairs)], lsem.at[3]),
+        pltpu.make_async_copy(regw_ref, wraw, lsem.at[3]),
     ]
-    for load in loads:
+    for load in loads[:3]:
         load.start()
 
     barrier = pltpu.get_barrier_semaphore()
@@ -50,9 +53,10 @@
     for other in greeted:
         pl.semaphore_signal(barrier, inc=1, device_id=other, device_id_type=MESH)
 
+    wbuf[pairs] = jnp.zeros_like(wbuf[pairs])
+    load_x.wait()
     for r in range(rows_here):
         xb[:, r * columns : (r + 1) * columns] = x_ref[r].astype(jnp.bfloat16)
-    wbuf[pairs] = jnp.zeros_like(wbuf[pairs])
     for c in range(channels // columns):
         row = jnp.broadcast_to(diff_ref[:, c * columns : (c + 1) * columns], (columns, columns))
         rate[c * columns : (c + 1) * columns, :] = row.T
@@ -67,10 +71,17 @@
 
     below = (s, lax.rem(t + 1, tiles))
     above = (s, lax.rem(t + tiles - 1, tiles))
-    halos = [
-        send(xb.at[:, pl.ds(cells - edge, edge)], halo.at[0], hsend.at[0], hrecv.at[0], below),
-        send(xb.at[:, pl.ds(0, edge)], halo.at[1], hsend.at[1], hrecv.at[1], above),
-    ]
+    def halos(i):
+        return [
+            send(
+                xb.at[span(i), pl.ds(cells - edge, edge)], halo.at[0, span(i), :],
+                hsend.at[0, i], hrecv.at[0, i], below,
+            ),
+            send(
+                xb.at[span(i), pl.ds(0, edge)], halo.at[1, span(i), :],
+                hsend.at[1, i], hrecv.at[1, i], above,
+            ),
+        ]
 
     def span(i):
         return pl.ds(pl.multiple_of(i * chunk, chunk), chunk)
@@ -110,10 +121,10 @@
         held = tuple(o for o in range(2 * REACH + 1) if o != REACH)
 
     def first(i):
-        return pl.ds(pl.multiple_of(i * chunk, half), half)
+        return pl.ds(pl.multiple_of(i * chunk, 8), part)
 
     def second(i):
-        return pl.ds(pl.multiple_of(i * chunk + half, half), half)
+        return pl.ds(pl.multiple_of(i * chunk + part, 8), chunk - part)
 
     def relay(n, i, src, dst, part, where):
         return send(
@@ -167,6 +178,7 @@
     loads[0].wait()
     loads[1].wait()
     loads[2].wait()
+    loads[3].start()
 
     def phase_a(i, carry):
         @pl.when(s == 0)
@@ -190,10 +202,13 @@
 
         return carry
 
-    for copy in halos:
-        copy.start()
+    def send_halos(i, carry):
+        for copy in halos(i):
+            copy.start()
+        return carry
+
+    lax.fori_loop(0, count, send_halos, 0)
     lax.fori_loop(0, count, phase_a, 0)
-    loads[3].wait()
     blocks = {slot: block_of(slot) for slot in (own,) + held}
 
     def add_to(which, landed, i):
@@ -263,7 +278,7 @@
         lax.fori_loop(0, chunk // 16, block, 0)
 
     def finish(i):
-        dims = (((1,), (1,)), ((), ()))
+        dims = (((1,), (0,)), ((), ()))
         total = lax.dot_general(
             fbuf[span(i), :], wbuf[blocks[own]], dims, preferred_element_type=jnp.float32
         )
@@ -277,53 +292,88 @@
                 mask_ref[r] == 1, out_ref[r, span(i), :] + here, x_ref[r, span(i), :]
             )
 
+    late = jnp.where((s == 1) | (s == 2), EXTRA, 0)
+
+    def store(i):
+        return pltpu.make_async_copy(
+            out_ref.at[:, span(i), :], result_ref.at[:, span(i), :], osem.at[i]
+        )
+
+    ahead = (s == 0) | (s == 3)
+    per = -(-pairs // 3)
+
+    def turn(k):
+        @pl.when(k < pairs)
+        def _():
+            wbuf[k] = wraw[k].T
+
+    def spread(i):
+        for copy in halos(i):
+            copy.wait_recv()
+        diffuse(i)
+
     def phase_b(i, carry):
+        @pl.when((i < count) & ahead)
+        def _():
+            spread(i)
+
         @pl.when(i < count)
         def _():
             forcing(i)
 
-        @pl.when((i >= 1) & (i < count + 1))
-        def _():
-            if paired:
-                one = gather1(i - 1)
-                two = gather2(i - 1)
+        @pl.when(i == 0)
+        def _():
+            loads[3].wait()
+
+        @pl.when(i < 3)
+        def _():
+            for k in range(per):
+                turn(i * per + k)
+
+        @pl.when((i < count) & jnp.logical_not(ahead))
+        def _():
+            spread(i)
+
+        j1 = i - 1 - late
+        j2 = j1 - 1
+        j3 = j1 - 2
+
+        if paired:
+            @pl.when((j1 >= 0) & (j1 < count))
+            def _():
+                one = gather1(j1)
+                two = gather2(j1)
                 one[1].wait_recv()
                 two[0].start()
                 two[1].start()
                 one[2].wait_recv()
                 two[2].start()
 
-        @pl.when(i == 2)
-        def _():
-            for copy in halos:
-                copy.wait_recv()
-
-        @pl.when((i >= 2) & (i < count + 2))
-        def _():
-            if paired:
-                two = gather2(i - 2)
-                three = gather3(i - 2)
+            @pl.when((j2 >= 0) & (j2 < count))
+            def _():
+                two = gather2(j2)
+                three = gather3(j2)
                 two[1].wait_recv()
                 three[0].start()
                 two[2].wait_recv()
                 three[1].start()
-            diffuse(i - 2)
-
-        @pl.when(i >= 3)
+
+        @pl.when((j3 >= 0) & (j3 < count))
         def _():
             if paired:
-                gather1(i - 3)[0].wait_recv()
-                gather2(i - 3)[0].wait_recv()
-                for copy in gather3(i - 3):
+                gather1(j3)[0].wait_recv()
+                gather2(j3)[0].wait_recv()
+                for copy in gather3(j3):
                     copy.wait_recv()
             else:
-                for copy in gather1(i - 3):
+                for copy in gather1(j3):
                     copy.wait_recv()
-            finish(i - 3)
+            finish(j3)
+            store(j3).start()
 
         return carry
 
-    lax.fori_loop(0, count + 3, phase_b, 0)
+    lax.fori_loop(0, count + 3 + EXTRA, phase_b, 0)
 
     def drain(i, carry):
         for section in range(slots):
@@ -331,13 +381,12 @@
             def _():
                 for copy in out_copies(section, i):
                     copy.wait_send()
-        for copy in gather1(i) + gather2(i) + gather3(i):
+        for copy in gather1(i) + gather2(i) + gather3(i) + halos(i):
             copy.wait_send()
+        store(i).wait()
         return carry
 
     lax.fori_loop(0, count, drain, 0)
-    for copy in halos:
-        copy.wait_send()
 
 
 def shards(slots, tiles, coupled_state, diffusivity, coupling, regrid_weights, source_offsets, sea_mask):
@@ -355,12 +404,15 @@
     result = pl.pallas_call(
         functools.partial(body, slots, tiles, chunk),
         out_shape=jax.ShapeDtypeStruct((rows_here, channels, columns), jnp.float32),
-        in_specs=[vmem, vmem, anyspace, anyspace, smem, vmem],
-        out_specs=vmem,
+        in_specs=[anyspace, vmem, anyspace, anyspace, smem, vmem],
+        out_specs=anyspace,
         scratch_shapes=[
+            pltpu.VMEM((rows_here, channels, columns), jnp.float32),
+            pltpu.VMEM((rows_here, channels, columns), jnp.float32),
             pltpu.VMEM((channels, cells), low),
             pltpu.VMEM((channels, columns), jnp.float32),
             pltpu.VMEM((3, channels, channels), low),
+            pltpu.VMEM((pairs, cells, cells), low),
             pltpu.VMEM((pairs + 1, cells, cells), low),
             pltpu.VMEM((held, channels, cells), low),
             pltpu.VMEM((3, channels, cells), low),
@@ -369,11 +421,12 @@
             pltpu.VMEM((2, channels, SWEEPS * columns), low),
             dma((3, count)),
             dma((3, count)),
-            dma((2,)),
-            dma((2,)),
+            dma((2, count)),
+            dma((2, count)),
             dma((8, count)),
             dma((8, count)),
-            dma((4,)),
+            dma((5,)),
+            dma((count,)),
         ],
         compiler_params=pltpu.CompilerParams(
             collective_id=0, has_side_effects=True, vmem_limit_bytes=60 * 1024 * 1024

time: 86.4 us -> 72.3 us (0.84)
  Pallas kernels: 83.3 us -> 68.6 us
    pallas_call x1, Pallas kernels: 83.3 us -> 68.6 us  [shards(): pl.pallas_call(functools.partial(body, slots, tiles, chunk), out_shape=ja...]
where the time goes in v2:
time: 72.3 us; the launch traced here: 71.5 us
  Pallas kernels  68.6 us (95%)
  local copies, waits for them, and re-layouts  2.94 us (4%)
    pallas_call x1, Pallas kernels, shards(): pl.pallas_call(functools.partial(body, slots, tiles, chunk), out_shape=ja...  68.6 us
    unnamed x1, local copies, waits for them, and re-layouts  2.94 us

profile of v2, /device:TPU:24, one launch (start us, length us, event | category | flops | bytes accessed | tf_op | source)
XLA Modules:
  0.0 71.5 jit_solution(1503788133780678079)
XLA Ops:
  0.0 68.6 %exchange.1 = f32[6,640,128]{2,1,0:T(8,128)} custom-call(f32[6,640,128]{2,1,0:T(8,128)} %bitcast.13, f32[1,640]{1,0:T(1,128)} %diff_ref.1, bf16[4,640,640]{2,1,0:T(8,128)(2,1)} %bitcast.12, bf16[6,768,768]{2,1,0:T(8,128)(2,1)} %bitcast.11, s32[1,6]{1,0:T(1,128)} %bitcast.15, s32[6,1,128]{2,1,0:T(1,128)} %bitcast.14), custom_call_target="tpu_custom_call" | custom-call | tf_op jit(solution)/shard_map/exchange/pallas_call | solution.py:404
  68.6 2.9 %copy.8 = f32[1,640,6,128]{3,1,2,0:T(8,128)} copy(f32[1,640,6,128]{3,1,2,0:T(8,128)} %bitcast.10) | data formatting | bytes 3932160
